TPU v7x, 32 devices: a whole 2x2x4 slice. The times are simulated.
32 devices in a mesh: lat: 2 (over x), lon: 8 (over z, y), grp: 2 (over core).
Axes of the slice: x: 2, y: 2, z: 4, core: 2. Of those that a mesh axis runs over, the one named last changes fastest.
Arguments:
- teacher_in: bfloat16 [2, 48, 96, 512], P('grp', 'lat', 'lon'), may hold values from -6 to 6
- student_in: bfloat16 [2, 48, 96, 256], P('grp', 'lat', 'lon'), may hold values from -6 to 6
- regions: int32 [2, 48, 96], P(None, 'lat', 'lon'), may hold values from 0 to 2
- t_qkv: bfloat16 [2, 512, 1536], replicated, may hold values from -0.25 to 0.25
- t_out: bfloat16 [2, 512, 512], replicated, may hold values from -0.25 to 0.25
- s_qkv: bfloat16 [2, 256, 768], replicated, may hold values from -0.375 to 0.375
- s_out: bfloat16 [2, 256, 256], replicated, may hold values from -0.375 to 0.375
- s_proj: bfloat16 [256, 512], replicated, may hold values from -0.375 to 0.375
Outputs:
- teacher_out: bfloat16 [2, 48, 96, 512], P('grp', 'lat', 'lon')
- student_grad: float32 [2, 48, 96, 256], P('grp', 'lat', 'lon')
All inputs are finite; a program needn't handle non-finite values.
Results may differ from a plain program's by a relative error of at most 0.02.
Values may be sent and summed in bfloat16 or wider, within the bound.
A program may use at most 128 MiB of HBM per device.

v0:
```python
import jax
import jax.numpy as jnp
from jax import lax
from jax.sharding import PartitionSpec as P

HEADS_T = 8
HEADS_S = 4


logit_scale = 10.0
eps = 1e-06


def from_partner(block, axis, stride):
    count = lax.axis_size(axis)
    route = []
    for low in range(count):
        high = low | 1 << stride
        if high != low and high < count:
            route += [(low, high), (high, low)]
    return lax.ppermute(block, axis, route)


def padded(shard, sides, width):
    for axis, dim in sides:
        size, length = (lax.axis_size(axis), shard.shape[dim])
        up = [(i, (i + 1) % size) for i in range(size)]
        down = [(j, i) for i, j in up]
        last = lax.slice_in_dim(shard, length - width, length, axis=dim)
        first = lax.slice_in_dim(shard, 0, width, axis=dim)
        before = lax.ppermute(last, axis, up)
        after = lax.ppermute(first, axis, down)
        shard = jnp.concatenate([before, shard, after], axis=dim)
    return shard


def to_bands(source):
    height, breadth = (source.shape[0], source.shape[1])
    return source.reshape((height // 12, 12 * breadth) + source.shape[2:])


def column_blocks(breadth):
    return jnp.tile(jnp.arange(breadth, dtype=jnp.int32) // 6, 12)


def head_split(source, head_count):
    bands, count, channels = source.shape
    heads = source.reshape(bands, count, head_count, channels // head_count)
    scale = lax.rsqrt(jnp.sum(jnp.square(heads.astype(jnp.float32)), axis=3) + eps)
    return (heads, scale.transpose(0, 2, 1))


def band_attend(
    queries, key_parts, value_parts, reg_query, reg_parts, col_query, col_parts, head_count
):
    bands, nquery, channels = queries.shape
    q_heads, scale_q = head_split(queries, head_count)
    exponents = []
    for key_rows, reg_key, col_key in zip(key_parts, reg_parts, col_parts):
        k_heads, scale_k = head_split(key_rows, head_count)
        products = jnp.einsum(
            "bqhd,bkhd->bhqk", q_heads, k_heads, preferred_element_type=jnp.float32
        )
        scores = logit_scale * products * scale_q[:, :, :, None] * scale_k[:, :, None, :]
        allowed = (reg_query[:, :, None] == reg_key[:, None, :]) & (
            col_query[None, :, None] == col_key[None, None, :]
        )
        exponents.append(jnp.where(allowed[:, None], jnp.exp(scores), jnp.zeros((), jnp.float32)))
    denominator = exponents[0].sum(axis=3, keepdims=True)
    for extra in exponents[1:]:
        denominator = denominator + extra.sum(axis=3, keepdims=True)
    safe = jnp.where(denominator > 0, denominator, jnp.ones((), jnp.float32))
    blended = jnp.zeros((bands, nquery, head_count, channels // head_count), jnp.float32)
    for exponent, value_rows in zip(exponents, value_parts):
        weights = (exponent / safe).astype(jnp.bfloat16)
        v_heads = value_rows.reshape(bands, value_rows.shape[1], head_count, channels // head_count)
        blended = blended + jnp.einsum(
            "bhqk,bkhd->bqhd", weights, v_heads, preferred_element_type=jnp.float32
        )
    return blended.astype(jnp.bfloat16).reshape(bands, nquery, channels)


def project(source, matrix):
    channels = source.shape[-1]
    flat = source.reshape(-1, channels).astype(jnp.bfloat16)
    result = jnp.dot(flat, matrix, preferred_element_type=jnp.float32).astype(jnp.bfloat16)
    return result.reshape(source.shape[:-1] + (matrix.shape[1],))


def finish(source, attended, w_output):
    channels = source.shape[-1]
    output = jnp.dot(attended.reshape(-1, channels), w_output, preferred_element_type=jnp.float32)
    normed = output * lax.rsqrt(jnp.mean(output * output, axis=-1, keepdims=True) + eps)
    return (
        (source.reshape(-1, channels).astype(jnp.float32) + normed)
        .astype(jnp.bfloat16)
        .reshape(source.shape)
    )


def student_grad(student_in, reg_own, target, s_qkv, s_out, s_proj, head_count):
    levels, height, breadth, channels = student_in.shape
    reg_band = to_bands(reg_own.reshape(levels * height, breadth))
    col_ids = column_blocks(breadth)

    def loss_fn(inputs):
        hidden = inputs
        for layer_idx in range(s_qkv.shape[0]):
            weight = s_qkv[layer_idx]
            flat = hidden.reshape(levels * height, breadth, channels)
            queries = to_bands(project(flat, weight[:, :channels]))
            key_rows = to_bands(project(flat, weight[:, channels : 2 * channels]))
            value_rows = to_bands(project(flat, weight[:, 2 * channels :]))
            attended = band_attend(
                queries,
                [key_rows],
                [value_rows],
                reg_band,
                [reg_band],
                col_ids,
                [col_ids],
                head_count,
            )
            hidden = finish(
                hidden, attended.reshape(levels, height, breadth, channels), s_out[layer_idx]
            )
        predicted = jnp.dot(
            hidden.reshape(-1, channels), s_proj, preferred_element_type=jnp.float32
        )
        residual = predicted - target.reshape(-1, target.shape[-1]).astype(jnp.float32)
        return 0.5 * jnp.sum(residual * residual)

    loss_value, pullback = jax.vjp(loss_fn, student_in.astype(jnp.float32))
    return pullback(jnp.ones((), jnp.float32))[0]


def in_pairs(source):
    return source.reshape((source.shape[0] // 2, 2) + source.shape[1:])


def shards(teacher_in, student_in, regions, t_qkv, t_out, s_qkv, s_out, s_proj):
    height, breadth, channels = (teacher_in.shape[1], teacher_in.shape[2], teacher_in.shape[3])
    own_level = lax.axis_index("grp")
    reg_own = lax.dynamic_index_in_dim(regions, own_level, 0, keepdims=True)
    reg_other = lax.dynamic_index_in_dim(regions, 1 - own_level, 0, keepdims=True)
    first = t_qkv[0]
    queries = project(teacher_in[0], first[:, :channels])
    pair_rows = project(teacher_in[0], first[:, channels:])
    pair_far = from_partner(pair_rows, "grp", 0)
    col_ids = column_blocks(breadth)
    reg_near = to_bands(reg_own[0])
    reg_far = to_bands(reg_other[0])
    attended = band_attend(
        to_bands(queries),
        [to_bands(pair_rows[..., :channels]), to_bands(pair_far[..., :channels])],
        [to_bands(pair_rows[..., channels:]), to_bands(pair_far[..., channels:])],
        reg_near,
        [reg_near, reg_far],
        col_ids,
        [col_ids, col_ids],
        HEADS_T,
    )
    hidden_a = finish(teacher_in, attended.reshape(1, height, breadth, channels), t_out[0])
    second = t_qkv[1]
    queries = project(hidden_a[0], second[:, :channels])
    payload = project(hidden_a[0], second[:, channels:])
    reg_flat = reg_own[0]
    load_ext, reg_ext = (
        padded(in_pairs(payload), (("lat", 0), ("lon", 2)), 3),
        padded(in_pairs(reg_flat), (("lat", 0), ("lon", 2)), 3),
    )
    tall = height + 12
    wide = breadth + 6
    pair_ext = load_ext.reshape(tall, wide, 2 * channels)
    reg_ext = reg_ext.reshape(tall, wide)
    global_rows = lax.axis_index("lat") * height + jnp.arange(tall, dtype=jnp.int32) - 6
    inside = (global_rows >= 0) & (global_rows < height * lax.axis_size("lat"))
    reg_ext = jnp.where(inside[:, None], reg_ext, -1)
    query_ext = jnp.pad(queries, ((6, 6), (3, 3), (0, 0)))
    reg_query = jnp.pad(reg_flat, ((6, 6), (3, 3)), constant_values=-1)
    col_ext = column_blocks(wide)
    attended = band_attend(
        to_bands(query_ext),
        [to_bands(pair_ext[..., :channels])],
        [to_bands(pair_ext[..., channels:])],
        to_bands(reg_query),
        [to_bands(reg_ext)],
        col_ext,
        [col_ext],
        HEADS_T,
    )
    attended = attended.reshape(1, tall, wide, channels)[:, 6 : 6 + height, 3 : 3 + breadth]
    teacher_out = finish(hidden_a, attended, t_out[1])
    gradient = student_grad(student_in, reg_own, teacher_out, s_qkv, s_out, s_proj, HEADS_S)
    return (teacher_out, gradient)


def solution(mesh):
    return jax.shard_map(
        shards,
        mesh=mesh,
        in_specs=(
            P("grp", "lat", "lon", None),
            P("grp", "lat", "lon", None),
            P(None, "lat", "lon"),
            P(),
            P(),
            P(),
            P(),
            P(),
        ),
        out_specs=(P("grp", "lat", "lon", None), P("grp", "lat", "lon", None)),
        check_vma=False,
    )
```

profile of v0, /device:TPU:0, one launch (start us, length us, event | category | flops | bytes accessed | tf_op | source)
XLA Modules:
  0.0 145.5 jit_solution(15542205626826520826)
XLA Ops:
  0.6 1.1 copy.181
  1.8 3.3 %slice_bitcast_fusion = (bf16[512,1536]{1,0:T(8,128)(2,1)}, bf16[512,1536]{1,0:T(8,128)(2,1)S(1)}) fusion(bf16[2,512,1536]{2,1,0:T(8,128)(2,1)} %param.11), kind=kLoop, calls=%fused_computation.13 | loop fusion | bytes 6291456 | tf_op jit(solution)/shard_map/squeeze | solution.py:164
  5.8 1.2 copy.189
  7.7 2.5 %collective-permute-start.6 = (s32[3,2,12]{2,1,0:T(2,128)S(1)}, s32[3,2,12]{2,1,0:T(2,128)S(1)}, u32[]{:S(2)}, u32[]{:S(2)}) collective-permute-start(s32[3,2,12]{2,1,0:T(2,128)S(1)} %slice.131), channel_id=1, source_target_pairs={{16,0},{0,16},{17,1},{1,17},{18,2},{2,18},{19,3},{3,19},{20,4},{4,... | collective-permute-start | bytes 872 | tf_op jit(solution)/shard_map/ppermute | solution.py:32
  17.8 1.5 %select_reduce_fusion.1 = (f32[2,4,144]{2,1,0:T(4,128)S(1)}, f32[2,4,144,144]{2,3,1,0:T(8,128)S(1)}) fusion(pred[2,144,144]{1,2,0:T(8,128)(4,1)S(1)} %get-tuple-element.30, f32[2,4,144]{2,1,0:T(4,128)S(1)} %rsqrt_bitcast_fusion.5, f32[2,4,144]{2,1,0:T(4,128)S(1)} %broadcast_multiply_fusion.1, bf16[2,144,4,64]{1,3,2,0:T(8,128)(2,1)} %copy-done.35, ...), kind=kOutput, calls=%fused_computation.111 | convolution fusion | flops 21896064 | bytes 1013760 | tf_op jit(solution)/shard_map/jvp(bqhd,bkhd->bhqk)/dot_general | solution.py:61
  21.5 1.2 copy.218
  22.9 1.3 multiply_reduce_fusion.13
  25.7 1.9 %fusion.58 = f32[2,8,144,144]{2,3,1,0:T(8,128)} fusion(bf16[2,144,8,64]{1,3,2,0:T(8,128)(2,1)S(1)} %copy.184, bf16[2,144,8,64]{3,2,1,0:T(8,128)(2,1)S(1)} %reshape_reshape.28), kind=kOutput, calls=%fused_computation.125 | convolution fusion | flops 42467328 | bytes 1916928 | tf_op jit(solution)/shard_map/bqhd,bkhd->bhqk/dot_general | solution.py:61
  34.0 1.2 copy.225
  35.5 1.8 %multiply_reduce_fusion.12 = (f32[288]{0:T(512)S(1)}, f32[288,256]{1,0:T(8,128)}) fusion(bf16[288,256]{1,0:T(8,128)(2,1)S(1)} %reshape.416, bf16[2,256,256]{2,1,0:T(8,128)(2,1)} %param.14), kind=kOutput, calls=%fused_computation.173 | convolution fusion | flops 37895904 | bytes 574592 | tf_op jit(solution)/shard_map/jvp()/dot_general | solution.py:92
  39.1 5.1 %collective-permute-start.8 = (s32[18,2,3]{2,1,0:T(2,128)S(1)}, s32[18,2,3]{2,1,0:T(2,128)S(1)}, u32[]{:S(2)}, u32[]{:S(2)}) collective-permute-start(s32[18,2,3]{2,1,0:T(2,128)S(1)} %get-tuple-element.33), channel_id=1, source_target_pairs={{2,0},{4,2},{6,4},{8,6},{10,8},{12,10},{14,12},{0,14},{3,1},{5,3},... | collective-permute-start | bytes 1304 | tf_op jit(solution)/shard_map/ppermute | solution.py:32
  45.7 5.0 %collective-permute-done.7 = s32[18,2,3]{2,1,0:T(2,128)S(1)} collective-permute-done((s32[18,2,3]{2,1,0:T(2,128)S(1)}, s32[18,2,3]{2,1,0:T(2,128)S(1)}, u32[]{:S(2)}, u32[]{:S(2)}) %collective-permute-start.7) | collective-permute-done | bytes 464 | tf_op jit(solution)/shard_map/ppermute | solution.py:31
  53.1 1.2 reshape_reshape.30
  54.2 2.9 %fusion.3 = (f32[2,8,144]{2,1,0:T(8,128)S(1)}, f32[2,8,144]{2,1,0:T(8,128)S(1)}, f32[2,8,144,144]{2,3,1,0:T(8,128)S(1)}) fusion(f32[2,8,144]{2,1,0:T(8,128)S(1)} %copy.193, f32[2,8,144]{2,1,0:T(8,128)S(1)} %copy.186, pred[2,144,144]{1,2,0:T(8,128)(4,1)S(1)} %copy-done.63, f32[2,8,144]{2,1,0:T(8,128)S(1)} %copy.187, f32[2,8,144,144]{2,3,1,0:T(8,128)} %fusion.58, ...), kind=kOutput, calls=%fused_computation.11 | convolution fusion | flops 45116928 | bytes 3373056 | tf_op jit(solution)/shard_map/bqhd,bkhd->bhqk/dot_general | solution.py:61
  57.2 1.1 fusion.28
  60.0 1.6 %multiply_reduce_fusion.10 = (f32[288]{0:T(512)S(1)}, f32[288,512]{1,0:T(8,128)S(1)}) fusion(bf16[288,512]{1,0:T(8,128)(2,1)S(1)} %reshape_reshape_reshape.7, bf16[2,512,512]{2,1,0:T(8,128)(2,1)} %param.12), kind=kOutput, calls=%fused_computation.143 | convolution fusion | flops 151289568 | bytes 1410176 | tf_op jit(solution)/shard_map/dot_general | solution.py:92
  64.5 1.5 %collective-permute-start.1 = (bf16[3,2,12,1024]{3,2,1,0:T(8,128)(2,1)}, bf16[3,2,12,1024]{3,2,1,0:T(8,128)(2,1)}, u32[]{:S(2)}, u32[]{:S(2)}) collective-permute-start(bf16[3,2,12,1024]{3,2,1,0:T(8,128)(2,1)} %slice.122), channel_id=1, source_target_pairs={{0,16},{16,0},{1,17},{17,1},{2,18},{18,2},{3,19},{19,3},{4,20},{20... | collective-permute-start | bytes 442376 | tf_op jit(solution)/shard_map/ppermute | solution.py:31
  66.9 1.2 reshape_reshape.31
  68.1 1.6 %slice.124 = bf16[3,2,12,1024]{3,2,1,0:T(8,128)(2,1)} reshape(bf16[72,1024]{1,0:T(8,128)(2,1)} %get-tuple-element.26) | data formatting | bytes 294912 | tf_op jit(solution)/shard_map/slice | solution.py:30
  71.5 4.0 %collective-permute-done.2 = bf16[3,2,12,1024]{3,2,1,0:T(8,128)(2,1)S(1)} collective-permute-done((bf16[3,2,12,1024]{3,2,1,0:T(8,128)(2,1)}, bf16[3,2,12,1024]{3,2,1,0:T(8,128)(2,1)S(1)}, u32[]{:S(2)}, u32[]{:S(2)}) %collective-permute-start.2) | collective-permute-done | bytes 147488 | tf_op jit(solution)/shard_map/ppermute | solution.py:32
  76.7 1.1 fusion.152
  77.8 2.0 %collective-permute-start.3 = (bf16[18,2,3,1024]{3,2,1,0:T(4,128)(2,1)}, bf16[18,2,3,1024]{3,2,1,0:T(4,128)(2,1)}, u32[]{:S(2)}, u32[]{:S(2)}) collective-permute-start(bf16[18,2,3,1024]{3,2,1,0:T(4,128)(2,1)} %get-tuple-element.20), channel_id=1, source_target_pairs={{0,2},{2,4},{4,6},{6,8},{8,10},{10,12},{12,14},{14,0},{1,3},{3,5},... | collective-permute-start | bytes 663560 | tf_op jit(solution)/shard_map/ppermute | solution.py:31
  81.2 1.5 %multiply_reduce_fusion.1 = f32[3,216,8]{2,1,0:T(8,128)} fusion(bf16[3,216,8,64]{3,2,1,0:T(8,128)(2,1)S(1)} %reshape_reshape.33), kind=kLoop, calls=%fused_computation.4 | loop fusion | flops 990144 | bytes 684288 | tf_op jit(solution)/shard_map/reduce_sum | solution.py:49
  82.7 1.1 copy.206
  83.8 6.7 %collective-permute-done.4 = bf16[18,2,3,1024]{3,2,1,0:T(4,128)(2,1)} collective-permute-done((bf16[18,2,3,1024]{3,2,1,0:T(4,128)(2,1)}, bf16[18,2,3,1024]{3,2,1,0:T(4,128)(2,1)}, u32[]{:S(2)}, u32[]{:S(2)}) %collective-permute-start.4) | collective-permute-done | bytes 221216 | tf_op jit(solution)/shard_map/ppermute | solution.py:32
  90.5 2.1 %pad_maximum_fusion = bf16[18,2,18,1024]{3,2,1,0:T(8,128)(2,1)S(1)} fusion(bf16[18,2,3,1024]{3,2,1,0:T(4,128)(2,1)} %collective-permute-done.4, bf16[18,2,12,1024]{3,2,1,0:T(8,128)(2,1)S(1)} %copy-done.14, bf16[18,2,3,1024]{3,2,1,0:T(4,128)(2,1)} %collective-permute-done.3), kind=kLoop, calls=%fused_computation.12 | loop fusion | flops 3981312 | bytes 2654208 | tf_op jit(solution)/shard_map/concatenate | solution.py:33
  92.6 1.4 fusion.151
  94.0 1.9 %reshape_reshape.34 = bf16[3,216,8,64]{3,2,1,0:T(8,128)(2,1)S(1)} reshape(bf16[36,18,512]{2,1,0:T(8,128)(2,1)} %get-tuple-element.19) | data formatting | bytes 1327104 | tf_op jit(solution)/shard_map/reshape;reshape | solution.py:48
  95.9 1.5 %multiply_reduce_fusion = f32[3,216,8]{2,1,0:T(8,128)} fusion(bf16[3,216,8,64]{3,2,1,0:T(8,128)(2,1)S(1)} %reshape_reshape.34), kind=kLoop, calls=%fused_computation.3 | loop fusion | flops 990144 | bytes 684288 | tf_op jit(solution)/shard_map/reduce_sum | solution.py:49
  97.3 1.1 copy.207
  98.5 4.5 %fusion = (f32[3,8,216]{2,1,0:T(8,128)S(1)}, f32[3,8,216,216]{2,3,1,0:T(8,128)}) fusion(f32[3,8,216]{2,1,0:T(8,128)S(1)} %get-tuple-element.69, f32[3,8,216]{2,1,0:T(8,128)S(1)} %get-tuple-element.70, pred[3,216,216]{1,2,0:T(8,128)(4,1)} %compare_and_fusion, bf16[3,216,8,64]{3,2,1,0:T(8,128)(2,1)S(1)} %reshape_reshape.34, ...), kind=kOutput, calls=%fused_computation.2 | convolution fusion | flops 147801024 | bytes 6008256 | tf_op jit(solution)/shard_map/bqhd,bkhd->bhqk/dot_general | solution.py:61
  103.0 1.9 %reshape_reshape.32 = bf16[3,216,8,64]{3,2,1,0:T(8,128)(2,1)S(1)} reshape(bf16[36,18,512]{2,1,0:T(8,128)(2,1)} %get-tuple-element.18) | data formatting | bytes 1327104 | tf_op jit(solution)/shard_map/reshape;reshape | solution.py:76
  105.0 4.8 %fusion.10 = bf16[3,216,8,64]{1,3,2,0:T(8,128)(2,1)S(1)} fusion(f32[3,8,216,216]{2,3,1,0:T(8,128)} %get-tuple-element.50, f32[3,8,216]{2,1,0:T(8,128)S(1)} %compare_select_fusion, f32[3,8,216]{2,1,0:T(8,128)S(1)} %copy-done.82, f32[3,8,216]{2,1,0:T(8,128)S(1)} %copy-done.84, pred[3,216,216]{1,2,0:T(8,128)(4,1)S(1)} %copy-done.53, ...), kind=kOutput, calls=%fused_computation.30 | convolution fusion | flops 149257728 | bytes 6008256 | tf_op jit(solution)/shard_map/bhqk,bkhd->bqhd/dot_general | solution.py:77
  109.7 1.3 copy.210
  111.1 1.2 reshape_reshape.35
  112.5 1.5 %multiply_reduce_fusion.9 = (f32[288]{0:T(512)S(1)}, f32[288,512]{1,0:T(8,128)S(1)}) fusion(bf16[288,512]{1,0:T(8,128)(2,1)S(1)} %reshape.405, bf16[2,512,512]{2,1,0:T(8,128)(2,1)} %param.12), kind=kOutput, calls=%fused_computation.141 | convolution fusion | flops 151289568 | bytes 1410176 | tf_op jit(solution)/shard_map/dot_general | solution.py:92
  117.8 1.3 fusion.31
  119.2 1.6 %fusion.21 = (f32[2,4,144]{2,1,0:T(4,128)S(1)}, bf16[2,4,144,144]{2,3,1,0:T(8,128)(2,1)S(1)}) fusion(f32[2,4,144]{2,1,0:T(4,128)S(1)} %copy-done.93, pred[2,144,144]{1,2,0:T(8,128)(4,1)S(1)} %copy-done.19, f32[2,4,144]{2,1,0:T(4,128)S(1)} %copy-done.73, f32[2,4,144,144]{2,3,1,0:T(8,128)S(1)} %copy-done.8, f32[2,4,144]{2,1,0:T(4,128)S(1)} %copy-done.75, ...), kind=kOutput, calls=%fused_computation.50 | convolution fusion | flops 22559616 | bytes 1350144 | tf_op jit(solution)/shard_map/transpose(jvp(bhqk,bkhd->bqhd))/dot_general | solution.py:77
  122.1 1.4 fusion.36
  123.5 1.2 copy.236
  125.6 1.1 convolution_convert_fusion.19
  126.7 2.6 %fusion.34 = bf16[2,144,4,64]{1,3,2,0:T(8,128)(2,1)} fusion(bf16[2,144,4,64]{1,3,2,0:T(8,128)(2,1)} %copy-done.39, f32[2,4,144]{2,1,0:T(4,128)S(1)} %get-tuple-element.43, f32[2,4,144]{2,1,0:T(4,128)S(1)} %copy-done.73, bf16[2,144,4,64]{1,3,2,0:T(8,128)(2,1)S(1)} %copy-done.38, f32[2,144,4]{1,2,0:T(4,128)S(1)} %fusion.130, ...), kind=kOutput, calls=%fused_computation.76 | convolution fusion | flops 23261184 | bytes 1506816 | tf_op jit(solution)/shard_map/transpose(jvp(bqhd,bkhd->bhqk))/dot_general | solution.py:61
  129.3 1.2 copy.233
  133.7 1.2 copy.239
  137.4 1.4 fusion.38
  138.8 1.2 copy.244
  140.2 2.5 %fusion.40 = bf16[2,144,4,64]{1,3,2,0:T(8,128)(2,1)} fusion(bf16[2,144,4,64]{1,3,2,0:T(8,128)(2,1)S(1)} %copy-done.34, f32[2,4,144]{2,1,0:T(4,128)S(1)} %get-tuple-element.39, f32[2,4,144]{2,1,0:T(4,128)S(1)} %copy-done.69, bf16[2,144,4,64]{1,3,2,0:T(8,128)(2,1)S(1)} %copy-done.36, f32[2,144,4]{1,2,0:T(4,128)S(1)} %get-tuple-element.38, ...), kind=kOutput, calls=%fused_computation.82 | convolution fusion | flops 23261184 | bytes 1506816 | tf_op jit(solution)/shard_map/transpose(jvp(bqhd,bkhd->bhqk))/dot_general | solution.py:61
  142.7 1.2 copy.247
  (349 shorter events, 47.3 us)
Async XLA Ops:
  0.6 114.5 %copy-start = (bf16[256,512]{1,0:T(8,128)(2,1)S(1)}, bf16[256,512]{1,0:T(8,128)(2,1)}, u32[]{:S(2)}) copy-start(bf16[256,512]{1,0:T(8,128)(2,1)} %param.15) | copy-start | bytes 786436
  1.8 8.4 %copy-start.25 = (bf16[288,512]{1,0:T(8,128)(2,1)}, bf16[288,512]{1,0:T(8,128)(2,1)S(1)}, u32[]{:S(2)}) copy-start(bf16[288,512]{1,0:T(8,128)(2,1)S(1)} %reshape.400) | copy-start | bytes 884740
  7.0 43.9 %collective-permute-start = (bf16[24,12,1024]{2,0,1:T(8,128)(2,1)}, bf16[24,12,1024]{2,0,1:T(8,128)(2,1)}, u32[]{:S(2)}, u32[]{:S(2)}) collective-permute-start(bf16[24,12,1024]{2,0,1:T(8,128)(2,1)} %copy.189), channel_id=1, source_target_pairs={{0,1},{1,0},{2,3},{3,2},{4,5},{5,4},{6,7},{7,6},{8,9},{9,8},{10,11... | collective-permute-start | bytes 1769480 | tf_op jit(solution)/shard_map/ppermute | solution.py:21
  7.7 31.3 %collective-permute-start.6 = (s32[3,2,12]{2,1,0:T(2,128)S(1)}, s32[3,2,12]{2,1,0:T(2,128)S(1)}, u32[]{:S(2)}, u32[]{:S(2)}) collective-permute-start(s32[3,2,12]{2,1,0:T(2,128)S(1)} %slice.131), channel_id=1, source_target_pairs={{16,0},{0,16},{17,1},{1,17},{18,2},{2,18},{19,3},{3,19},{20,4},{4,... | collective-permute-start | bytes 872 | tf_op jit(solution)/shard_map/ppermute | solution.py:32
  10.2 28.7 %collective-permute-start.5 = (s32[3,2,12]{2,1,0:T(2,128)S(1)}, s32[3,2,12]{2,1,0:T(2,128)S(1)}, u32[]{:S(2)}, u32[]{:S(2)}) collective-permute-start(s32[3,2,12]{2,1,0:T(2,128)S(1)} %slice.129), channel_id=1, source_target_pairs={{0,16},{16,0},{1,17},{17,1},{2,18},{18,2},{3,19},{19,3},{4,20},{20... | collective-permute-start | bytes 872 | tf_op jit(solution)/shard_map/ppermute | solution.py:31
  14.3 10.4 %copy-start.9 = (bf16[256,768]{1,0:T(8,128)(2,1)}, bf16[256,768]{1,0:T(8,128)(2,1)S(1)}, u32[]{:S(2)}) copy-start(bf16[256,768]{1,0:T(8,128)(2,1)S(1)} %get-tuple-element.22) | copy-start | bytes 1179652
  15.9 4.5 %copy-start.29 = (bf16[2,144,4,64]{1,3,2,0:T(8,128)(2,1)}, bf16[2,144,4,64]{1,3,2,0:T(8,128)(2,1)S(1)}, u32[]{:S(2)}) copy-start(bf16[2,144,4,64]{1,3,2,0:T(8,128)(2,1)S(1)} %copy.216) | copy-start | bytes 442372
  16.3 3.0 %copy-start.33 = (bf16[2,144,4,64]{1,3,2,0:T(8,128)(2,1)}, bf16[2,144,4,64]{1,3,2,0:T(8,128)(2,1)S(1)}, u32[]{:S(2)}) copy-start(bf16[2,144,4,64]{1,3,2,0:T(8,128)(2,1)S(1)} %copy.213) | copy-start | bytes 442372
  16.4 2.9 %copy-start.55 = (f32[2,144,4]{1,2,0:T(4,128)}, f32[2,144,4]{1,2,0:T(4,128)S(1)}, u32[]{:S(2)}) copy-start(f32[2,144,4]{1,2,0:T(4,128)S(1)} %fusion.75) | copy-start | bytes 13828
  16.4 3.6 %copy-start.68 = (f32[2,4,144]{2,1,0:T(4,128)}, f32[2,4,144]{2,1,0:T(4,128)S(1)}, u32[]{:S(2)}) copy-start(f32[2,4,144]{2,1,0:T(4,128)S(1)} %rsqrt_bitcast_fusion.5) | copy-start | bytes 13828
  16.9 2.4 %copy-start.59 = (f32[2,144,4]{1,2,0:T(4,128)}, f32[2,144,4]{1,2,0:T(4,128)S(1)}, u32[]{:S(2)}) copy-start(f32[2,144,4]{1,2,0:T(4,128)S(1)} %fusion.73) | copy-start | bytes 13828
  17.0 3.0 %copy-start.70 = (f32[2,4,144]{2,1,0:T(4,128)}, f32[2,4,144]{2,1,0:T(4,128)S(1)}, u32[]{:S(2)}) copy-start(f32[2,4,144]{2,1,0:T(4,128)S(1)} %broadcast_multiply_fusion.1) | copy-start | bytes 13828
  17.8 39.4 %copy-start.18 = (pred[2,144,144]{1,2,0:T(8,128)(4,1)}, pred[2,144,144]{1,2,0:T(8,128)(4,1)S(1)}, u32[]{:S(2)}) copy-start(pred[2,144,144]{1,2,0:T(8,128)(4,1)S(1)} %get-tuple-element.30) | copy-start | bytes 124420
  19.3 2.2 %copy-start.5 = (f32[2,4,144,144]{2,3,1,0:T(8,128)}, f32[2,4,144,144]{2,3,1,0:T(8,128)S(1)}, u32[]{:S(2)}) copy-start(f32[2,4,144,144]{2,3,1,0:T(8,128)S(1)} %get-tuple-element.54) | copy-start | bytes 1990660
  30.2 2.7 %copy-start.31 = (bf16[2,144,4,64]{1,3,2,0:T(8,128)(2,1)}, bf16[2,144,4,64]{1,3,2,0:T(8,128)(2,1)S(1)}, u32[]{:S(2)}) copy-start(bf16[2,144,4,64]{1,3,2,0:T(8,128)(2,1)S(1)} %copy.223) | copy-start | bytes 442372
  31.8 2.2 %copy-start.7 = (f32[2,4,144,144]{2,3,1,0:T(8,128)}, f32[2,4,144,144]{2,3,1,0:T(8,128)S(1)}, u32[]{:S(2)}) copy-start(f32[2,4,144,144]{2,3,1,0:T(8,128)S(1)} %get-tuple-element.58) | copy-start | bytes 1990660
  33.1 4.2 %copy-start.1 = (bf16[2,4,144,144]{2,3,1,0:T(8,128)(2,1)}, bf16[2,4,144,144]{2,3,1,0:T(8,128)(2,1)S(1)}, u32[]{:S(2)}) copy-start(bf16[2,4,144,144]{2,3,1,0:T(8,128)(2,1)S(1)} %divide_convert_fusion.8) | copy-start | bytes 995332
  35.2 3.7 %copy-start.46 = (f32[2,8,144]{1,2,0:T(8,128)S(1)}, f32[2,8,144]{1,2,0:T(8,128)}, u32[]{:S(2)}) copy-start(f32[2,8,144]{1,2,0:T(8,128)} %rsqrt_bitcast_fusion.1) | copy-start | bytes 27652
  35.2 9.0 %copy-start.21 = (bf16[24,12,512]{2,1,0:T(8,128)(2,1)S(1)}, bf16[24,12,512]{2,1,0:T(8,128)(2,1)}, u32[]{:S(2)}) copy-start(bf16[24,12,512]{2,1,0:T(8,128)(2,1)} %get-tuple-element.24) | copy-start | bytes 884740
  37.3 6.9 %copy-start.89 = (f32[288]{0:T(512)}, f32[288]{0:T(512)S(1)}, u32[]{:S(2)}) copy-start(f32[288]{0:T(512)S(1)} %get-tuple-element.59) | copy-start | bytes 3460
  39.1 6.6 %collective-permute-start.8 = (s32[18,2,3]{2,1,0:T(2,128)S(1)}, s32[18,2,3]{2,1,0:T(2,128)S(1)}, u32[]{:S(2)}, u32[]{:S(2)}) collective-permute-start(s32[18,2,3]{2,1,0:T(2,128)S(1)} %get-tuple-element.33), channel_id=1, source_target_pairs={{2,0},{4,2},{6,4},{8,6},{10,8},{12,10},{14,12},{0,14},{3,1},{5,3},... | collective-permute-start | bytes 1304 | tf_op jit(solution)/shard_map/ppermute | solution.py:32
  44.2 6.5 %collective-permute-start.7 = (s32[18,2,3]{2,1,0:T(2,128)S(1)}, s32[18,2,3]{2,1,0:T(2,128)S(1)}, u32[]{:S(2)}, u32[]{:S(2)}) collective-permute-start(s32[18,2,3]{2,1,0:T(2,128)S(1)} %get-tuple-element.32), channel_id=1, source_target_pairs={{0,2},{2,4},{4,6},{6,8},{8,10},{10,12},{12,14},{14,0},{1,3},{3,5},... | collective-permute-start | bytes 1304 | tf_op jit(solution)/shard_map/ppermute | solution.py:31
  54.2 3.0 %copy-start.17 = (f32[2,8,144,144]{2,3,1,0:T(8,128)S(1)}, f32[2,8,144,144]{2,3,1,0:T(8,128)}, u32[]{:S(2)}) copy-start(f32[2,8,144,144]{2,3,1,0:T(8,128)} %fusion.58) | copy-start | bytes 3981316
  61.8 18.1 %copy-start.27 = (bf16[288,512]{1,0:T(8,128)(2,1)}, bf16[288,512]{1,0:T(8,128)(2,1)S(1)}, u32[]{:S(2)}) copy-start(bf16[288,512]{1,0:T(8,128)(2,1)S(1)} %add_convert_fusion.1) | copy-start | bytes 884740
  61.8 4.2 %copy-start.52 = (pred[216,216]{0,1:T(8,128)(4,1)S(1)}, pred[216,216]{0,1:T(8,128)(4,1)}, u32[]{:S(2)}) copy-start(pred[216,216]{0,1:T(8,128)(4,1)} %broadcast_compare_fusion) | copy-start | bytes 139972
  64.5 6.0 %collective-permute-start.1 = (bf16[3,2,12,1024]{3,2,1,0:T(8,128)(2,1)}, bf16[3,2,12,1024]{3,2,1,0:T(8,128)(2,1)}, u32[]{:S(2)}, u32[]{:S(2)}) collective-permute-start(bf16[3,2,12,1024]{3,2,1,0:T(8,128)(2,1)} %slice.122), channel_id=1, source_target_pairs={{0,16},{16,0},{1,17},{17,1},{2,18},{18,2},{3,19},{19,3},{4,20},{20... | collective-permute-start | bytes 442376 | tf_op jit(solution)/shard_map/ppermute | solution.py:31
  69.7 5.9 %collective-permute-start.2 = (bf16[3,2,12,1024]{3,2,1,0:T(8,128)(2,1)}, bf16[3,2,12,1024]{3,2,1,0:T(8,128)(2,1)S(1)}, u32[]{:S(2)}, u32[]{:S(2)}) collective-permute-start(bf16[3,2,12,1024]{3,2,1,0:T(8,128)(2,1)} %slice.124), channel_id=1, source_target_pairs={{16,0},{0,16},{17,1},{1,17},{18,2},{2,18},{19,3},{3,19},{20,4},{4,... | collective-permute-start | bytes 442376 | tf_op jit(solution)/shard_map/ppermute | solution.py:32
  77.8 12.7 %collective-permute-start.4 = (bf16[18,2,3,1024]{3,2,1,0:T(4,128)(2,1)}, bf16[18,2,3,1024]{3,2,1,0:T(4,128)(2,1)}, u32[]{:S(2)}, u32[]{:S(2)}) collective-permute-start(bf16[18,2,3,1024]{3,2,1,0:T(4,128)(2,1)} %get-tuple-element.21), channel_id=1, source_target_pairs={{2,0},{4,2},{6,4},{8,6},{10,8},{12,10},{14,12},{0,14},{3,1},{5,3},... | collective-permute-start | bytes 663560 | tf_op jit(solution)/shard_map/ppermute | solution.py:32
  77.8 12.7 %collective-permute-start.3 = (bf16[18,2,3,1024]{3,2,1,0:T(4,128)(2,1)}, bf16[18,2,3,1024]{3,2,1,0:T(4,128)(2,1)}, u32[]{:S(2)}, u32[]{:S(2)}) collective-permute-start(bf16[18,2,3,1024]{3,2,1,0:T(4,128)(2,1)} %get-tuple-element.20), channel_id=1, source_target_pairs={{0,2},{2,4},{4,6},{6,8},{8,10},{10,12},{12,14},{14,0},{1,3},{3,5},... | collective-permute-start | bytes 663560 | tf_op jit(solution)/shard_map/ppermute | solution.py:31
  81.2 9.3 %copy-start.14 = (bf16[18,2,12,1024]{3,2,1,0:T(8,128)(2,1)S(1)}, bf16[18,2,12,1024]{3,2,1,0:T(8,128)(2,1)}, u32[]{:S(2)}) copy-start(bf16[18,2,12,1024]{3,2,1,0:T(8,128)(2,1)} %copy-done.13) | copy-start | bytes 2654212
  98.5 4.5 %copy-start.81 = (f32[3,8,216]{2,1,0:T(8,128)}, f32[3,8,216]{2,1,0:T(8,128)S(1)}, u32[]{:S(2)}) copy-start(f32[3,8,216]{2,1,0:T(8,128)S(1)} %get-tuple-element.69) | copy-start | bytes 62212
  98.5 4.5 %copy-start.83 = (f32[3,8,216]{2,1,0:T(8,128)}, f32[3,8,216]{2,1,0:T(8,128)S(1)}, u32[]{:S(2)}) copy-start(f32[3,8,216]{2,1,0:T(8,128)S(1)} %get-tuple-element.70) | copy-start | bytes 62212
  116.7 2.4 %copy-start.8 = (f32[2,4,144,144]{2,3,1,0:T(8,128)S(1)}, f32[2,4,144,144]{2,3,1,0:T(8,128)}, u32[]{:S(2)}) copy-start(f32[2,4,144,144]{2,3,1,0:T(8,128)} %copy-done.7) | copy-start | bytes 1990660
  116.7 2.4 %copy-start.19 = (pred[2,144,144]{1,2,0:T(8,128)(4,1)S(1)}, pred[2,144,144]{1,2,0:T(8,128)(4,1)}, u32[]{:S(2)}) copy-start(pred[2,144,144]{1,2,0:T(8,128)(4,1)} %copy-done.18) | copy-start | bytes 124420
  116.7 2.4 %copy-start.32 = (bf16[2,144,4,64]{1,3,2,0:T(8,128)(2,1)S(1)}, bf16[2,144,4,64]{1,3,2,0:T(8,128)(2,1)}, u32[]{:S(2)}) copy-start(bf16[2,144,4,64]{1,3,2,0:T(8,128)(2,1)} %copy-done.31) | copy-start | bytes 442372
  116.7 2.4 %copy-start.73 = (f32[2,4,144]{2,1,0:T(4,128)S(1)}, f32[2,4,144]{2,1,0:T(4,128)}, u32[]{:S(2)}) copy-start(f32[2,4,144]{2,1,0:T(4,128)} %copy-done.72) | copy-start | bytes 13828
  116.7 2.4 %copy-start.75 = (f32[2,4,144]{2,1,0:T(4,128)S(1)}, f32[2,4,144]{2,1,0:T(4,128)}, u32[]{:S(2)}) copy-start(f32[2,4,144]{2,1,0:T(4,128)} %copy-done.74) | copy-start | bytes 13828
  116.7 2.4 %copy-start.93 = (f32[2,4,144]{2,1,0:T(4,128)S(1)}, f32[2,4,144]{2,1,0:T(4,128)}, u32[]{:S(2)}) copy-start(f32[2,4,144]{2,1,0:T(4,128)} %get-tuple-element.44) | copy-start | bytes 13828
  122.1 3.5 %copy-start.10 = (bf16[256,768]{1,0:T(8,128)(2,1)S(1)}, bf16[256,768]{1,0:T(8,128)(2,1)}, u32[]{:S(2)}) copy-start(bf16[256,768]{1,0:T(8,128)(2,1)} %copy-done.9) | copy-start | bytes 1179652
  123.5 3.2 %copy-start.58 = (f32[2,144,4]{1,2,0:T(4,128)S(1)}, f32[2,144,4]{1,2,0:T(4,128)}, u32[]{:S(2)}) copy-start(f32[2,144,4]{1,2,0:T(4,128)} %copy-done.57) | copy-start | bytes 13828
  129.3 2.2 %copy-start.4 = (f32[288,256]{1,0:T(8,128)S(1)}, f32[288,256]{1,0:T(8,128)}, u32[]{:S(2)}) copy-start(f32[288,256]{1,0:T(8,128)} %copy-done.3) | copy-start | bytes 884740
  129.3 2.2 %copy-start.45 = (bf16[288,256]{1,0:T(8,128)(2,1)S(1)}, bf16[288,256]{1,0:T(8,128)(2,1)}, u32[]{:S(2)}) copy-start(bf16[288,256]{1,0:T(8,128)(2,1)} %copy-done.44) | copy-start | bytes 442372
  132.6 2.5 %copy-start.12 = (bf16[256,768]{1,0:T(8,128)(2,1)S(1)}, bf16[256,768]{1,0:T(8,128)(2,1)}, u32[]{:S(2)}) copy-start(bf16[256,768]{1,0:T(8,128)(2,1)} %copy-done.11) | copy-start | bytes 1179652
  132.6 2.7 %copy-start.6 = (f32[2,4,144,144]{2,3,1,0:T(8,128)S(1)}, f32[2,4,144,144]{2,3,1,0:T(8,128)}, u32[]{:S(2)}) copy-start(f32[2,4,144,144]{2,3,1,0:T(8,128)} %copy-done.5) | copy-start | bytes 1990660
  132.7 2.7 %copy-start.30 = (bf16[2,144,4,64]{1,3,2,0:T(8,128)(2,1)S(1)}, bf16[2,144,4,64]{1,3,2,0:T(8,128)(2,1)}, u32[]{:S(2)}) copy-start(bf16[2,144,4,64]{1,3,2,0:T(8,128)(2,1)} %copy-done.29) | copy-start | bytes 442372
  132.7 2.7 %copy-start.69 = (f32[2,4,144]{2,1,0:T(4,128)S(1)}, f32[2,4,144]{2,1,0:T(4,128)}, u32[]{:S(2)}) copy-start(f32[2,4,144]{2,1,0:T(4,128)} %copy-done.68) | copy-start | bytes 13828
  132.7 2.7 %copy-start.71 = (f32[2,4,144]{2,1,0:T(4,128)S(1)}, f32[2,4,144]{2,1,0:T(4,128)}, u32[]{:S(2)}) copy-start(f32[2,4,144]{2,1,0:T(4,128)} %copy-done.70) | copy-start | bytes 13828
  132.7 2.7 %copy-start.92 = (f32[2,4,144]{2,1,0:T(4,128)S(1)}, f32[2,4,144]{2,1,0:T(4,128)}, u32[]{:S(2)}) copy-start(f32[2,4,144]{2,1,0:T(4,128)} %get-tuple-element.40) | copy-start | bytes 13828
  (55 other events, 70.2 us)
where the time goes:
time: 147 us; the launch traced here: 146 us
  local copies, waits for them, and re-layouts  51.9 us (35%)
  matrix products  45.5 us (31%)
  waiting for transfers between devices  16.8 us (11%)
  other arithmetic  16.5 us (11%)
  starting transfers between devices  12.2 us (8%)
  between operations  2.64 us (2%)
    dot_general x9, matrix products, band_attend(): jnp.einsum('bqhd,bkhd->bhqk', q_heads, k_heads, preferred_element_type=jn...  19.3 us
    dot_general x9, matrix products, band_attend(): jnp.einsum('bhqk,bkhd->bqhd', weights, v_heads, preferred_element_type=jn...  13.2 us
    ppermute x4, waiting for transfers between devices, padded(): after = lax.ppermute(first, axis, down)  11.5 us
    ppermute x4, starting transfers between devices, padded(): after = lax.ppermute(first, axis, down)  8.16 us
    unnamed x194, local copies, waits for them, and re-layouts  7.51 us
    dot_general x6, matrix products, finish(): jnp.dot(attended.reshape(-1, channels), w_output, preferred_element_type=...  6.65 us
    dot_general x16, matrix products, project(): jnp.dot(flat, matrix, preferred_element_type=jnp.float32)  5.81 us
    ppermute x4, waiting for transfers between devices, padded(): before = lax.ppermute(last, axis, up)  5.27 us
  transfers between devices with their start and end apart: 9, of which 5 were waited for; matrix products, arithmetic and copies ran while one was open for 26% of the time, Pallas kernels for 0%

commit v1 on v0

v1 whole, which is shorter than its diff:
```python
import functools

import jax
import jax.numpy as jnp
import numpy as np
from jax import lax
from jax.experimental import pallas as pl
from jax.experimental.pallas import tpu as pltpu
from jax.sharding import PartitionSpec as P

HEADS_T = 8
HEADS_S = 4
SCALE = 10.0
EPS = 1e-06
BF = jnp.bfloat16
F32 = jnp.float32
MESH = pl.DeviceIdType.MESH

ROWS, COLS, PADC = 24, 12, 16
TOK = ROWS * PADC
BAND = 12 * PADC
HALF = 6 * PADC
SIDE = 96
FEAT = 128
SEC_L, SEC_R, SEC_TL, SEC_BL, SEC_TR, SEC_BR = (
    (0, 80),
    (80, 80),
    (160, 32),
    (192, 32),
    (224, 32),
    (256, 32),
)
PACK = 288


def dot(a, b):
    return jnp.dot(a, b, preferred_element_type=F32)


def dot_nt(a, b):
    return lax.dot_general(a, b, (((1,), (1,)), ((), ())), preferred_element_type=F32)


def dot_tn(a, b):
    return lax.dot_general(a, b, (((0,), (0,)), ((), ())), preferred_element_type=F32)


def constants():
    gather = np.zeros((PACK, TOK), np.float32)

    def put(section, rows, cols):
        at = section[0]
        for row in rows:
            for col in cols:
                gather[at, row * PADC + col] = 1
                at += 1

    top, bottom = range(6), range(ROWS - 6, ROWS)
    first, last = range(3), range(COLS - 3, COLS)
    put(SEC_L, range(ROWS), last)
    put(SEC_R, range(ROWS), first)
    put(SEC_TL, bottom, last)
    put(SEC_BL, top, last)
    put(SEC_TR, bottom, first)
    put(SEC_BR, top, first)
    spread = np.zeros((PACK, PACK), np.float32)
    for band in range(3):
        for line in range(12):
            row = band * 12 + line - 6
            for side, (mid, above, below) in enumerate(
                ((SEC_L, SEC_TL, SEC_BL), (SEC_R, SEC_TR, SEC_BR))
            ):
                if row < 0:
                    source = above[0] + (row + 6) * 3
                elif row >= ROWS:
                    source = below[0] + (row - ROWS) * 3
                else:
                    source = mid[0] + row * 3
                for col in range(3):
                    spread[band * SIDE + side * 36 + line * 3 + col, source + col] = 1
    token_col = np.arange(BAND) % PADC
    win = token_col // 6
    same = (win[:, None] == win[None, :]).astype(np.float32)
    shifted = (token_col + 3) // 6
    side_win = np.full((SIDE,), 99)
    side_win[:36] = 0
    side_win[36:72] = 2
    keys = np.concatenate([shifted, side_win])
    same_shifted = (shifted[:, None] == keys[None, :]).astype(np.float32)
    heads = (np.arange(256)[:, None] // 64 == np.arange(256)[None, :] // 64).astype(np.float32)
    of_row = (np.arange(TOK)[:, None] // PADC == np.arange(128)[None, :]).astype(np.float32)
    of_col = (np.arange(TOK)[:, None] % PADC == np.arange(128)[None, :]).astype(np.float32)
    return (
        jnp.asarray(gather, BF),
        jnp.asarray(spread, BF),
        jnp.asarray(same, F32),
        jnp.asarray(same_shifted, F32),
        jnp.asarray(heads, BF),
        jnp.asarray(of_row, BF),
        jnp.asarray(of_col, F32),
    )


def inverse_norm(values, heads):
    square = (values * values).astype(BF)
    parts = [
        dot(square[:, at : at + 256], heads) for at in range(0, values.shape[1], 256)
    ]
    total = parts[0] if len(parts) == 1 else jnp.concatenate(parts, axis=1)
    return lax.rsqrt(total + EPS)


def pair_masks():
    lane = lax.broadcasted_iota(jnp.int32, (1, 128), 1)
    low = jnp.where(lane < 64, 1.0, 0.0).astype(F32)
    return low.astype(BF), (1.0 - low).astype(BF)


def attend_pair(q, k, v, bias):
    low, high = pair_masks()
    exp_e = jnp.exp(dot_nt(q, k * low) + bias).astype(BF)
    exp_o = jnp.exp(dot_nt(q, k * high) + bias).astype(BF)
    out_e = dot(exp_e, v * low + high)
    out_o = dot(exp_o, v * high + low)
    is_low = lax.broadcasted_iota(jnp.int32, out_e.shape, 1) < 64
    total = jnp.where(is_low, out_e, out_o)
    den = pltpu.roll(jnp.where(is_low, out_o, out_e), 64, 1)
    return (total / jnp.where(den > 0, den, 1.0)).astype(BF)


def attend_pair_back(q, k, v, grad, bias):
    masks = pair_masks()
    dq = dk = dv = None
    for mask in masks:
        k_own = k * mask
        exps = jnp.exp(dot_nt(k_own, q) + bias)
        den = jnp.sum(exps, axis=0, keepdims=True)
        weights = exps * (1.0 / jnp.where(den > 0, den, 1.0))
        d_weights = dot_nt(v * mask, grad)
        inner = jnp.sum(weights * d_weights, axis=0, keepdims=True)
        d_scores = (weights * (d_weights - inner)).astype(BF)
        q_part = dot_tn(d_scores, k_own)
        k_part = dot(d_scores, q * mask)
        v_part = dot(weights.astype(BF), grad * mask)
        dq = q_part if dq is None else dq + q_part
        dk = k_part if dk is None else dk + k_part
        dv = v_part if dv is None else dv + v_part
    return dq, dk, dv


def bias_of(f_query, f_key, same):
    return (dot_nt(f_query, f_key) * same - 1.0) * 1e30


def lanes(pair):
    return pl.ds(pl.multiple_of(pair * 128, 128), 128)


def band_rows(band, size=BAND):
    return pl.ds(pl.multiple_of(band * size, 16), size)


def normed(o):
    return lax.rsqrt(jnp.mean(o * o, axis=-1, keepdims=True) + EPS)


def kernel(
    n_lat,
    n_lon,
    x_ref,
    s_ref,
    reg_ref,
    tqkv,
    tout,
    sqkv,
    sout,
    sproj,
    gather,
    spread,
    same,
    same_shifted,
    heads,
    of_row,
    of_col,
    out_ref,
    grad_ref,
    pad_t,
    pad_s,
    reg_pad,
    xa,
    qa,
    ka,
    va,
    bias_a,
    bias_s,
    bias_b,
    att,
    hext,
    pack,
    side_in,
    side,
    kb,
    vb,
    hid,
    q_s,
    k_s,
    v_s,
    rq_s,
    rk_s,
    o_s,
    att_s,
    pred,
    da_s,
    dqkv,
    send,
    recv,
):
    lat, lon, grp = lax.axis_index("lat"), lax.axis_index("lon"), lax.axis_index("grp")
    right, left = lax.rem(lon + 1, n_lon), lax.rem(lon + n_lon - 1, n_lon)
    has_up, has_down = lat > 0, lat < n_lat - 1
    barrier = pltpu.get_barrier_semaphore()

    def greet(device):
        pl.semaphore_signal(barrier, inc=1, device_id=device, device_id_type=MESH)

    greet((lat, lon, 1 - grp))
    greet((lat, left, grp))
    greet((lat, right, grp))

    @pl.when(has_up)
    def _():
        for column in (left, lon, right):
            greet((lat - 1, column, grp))

    @pl.when(has_down)
    def _():
        for column in (left, lon, right):
            greet((lat + 1, column, grp))

    pad_t[...] = jnp.zeros_like(pad_t)
    pad_t[:, 0:COLS, :] = x_ref[...]
    pad_s[...] = jnp.zeros_like(pad_s)
    pad_s[:, 0:COLS, :] = s_ref[...]
    reg_pad[...] = jnp.zeros_like(reg_pad)
    reg_pad[0:ROWS, 0:COLS] = (reg_ref[grp] + 1).astype(F32)
    region = jnp.sum(
        dot(of_row[...], reg_pad[...].astype(BF)) * of_col[...], axis=1, keepdims=True
    )
    lane = lax.broadcasted_iota(jnp.int32, (TOK, FEAT), 1).astype(F32)
    feature = jnp.where((region == lane) & (region > 0.5), 1.0, 0.0).astype(BF)
    xa[0:TOK, 0:512] = pad_t[...].reshape(TOK, 512)
    xa[0:TOK, 512:640] = feature
    hext[HALF : HALF + TOK, 512:640] = feature
    hid[0] = pad_s[...].reshape(TOK, 256)

    @pl.when(jnp.logical_not(has_up))
    def _():
        hext[0:HALF, :] = jnp.zeros((HALF, 640), BF)
        for at, size in (SEC_TL, SEC_TR):
            side_in[at : at + size, :] = jnp.zeros((size, 640), BF)

    @pl.when(jnp.logical_not(has_down))
    def _():
        hext[HALF + TOK :, :] = jnp.zeros((HALF, 640), BF)
        for at, size in (SEC_BL, SEC_BR):
            side_in[at : at + size, :] = jnp.zeros((size, 640), BF)

    rows_near = has_up.astype(jnp.int32) + has_down.astype(jnp.int32)
    pl.semaphore_wait(barrier, 3 + 3 * rows_near)

    def copy_to(source, target, slot, device):
        return pltpu.make_async_remote_copy(
            src_ref=source,
            dst_ref=target,
            send_sem=send.at[slot],
            recv_sem=recv.at[slot],
            device_id=device,
            device_id_type=MESH,
        )

    to_partner = copy_to(xa.at[0:TOK], xa.at[TOK : 2 * TOK], 0, (lat, lon, 1 - grp))
    to_partner.start()

    w_a = tqkv.at[0]

    def project_keys(rows, source, weight, k_ref, v_ref, target):
        value = source[rows, 0:512]
        keys = dot(value, weight[:, 512:1024]).astype(BF).astype(F32)
        k_ref[target, :] = (keys * inverse_norm(keys, heads[...])).astype(BF)
        v_ref[target, :] = dot(value, weight[:, 1024:1536]).astype(BF)

    def project_queries(value, weight):
        q = dot(value, weight[:, 0:512]).astype(BF).astype(F32)
        return (q * (inverse_norm(q, heads[...]) * SCALE)).astype(BF)

    def own_a(band, carry):
        rows = band_rows(band)
        qa[rows, :] = project_queries(xa[rows, 0:512], w_a)
        project_keys(rows, xa, w_a, ka, va, rows)
        own = xa[rows, 512:640]
        bias = bias_of(own, own, same[...])
        bias_s[rows, :] = bias
        return carry

    lax.fori_loop(0, 2, own_a, 0)
    to_partner.wait()

    def far_a(band, carry):
        rows = band_rows(band + 2)
        project_keys(rows, xa, w_a, ka, va, rows)
        return carry

    lax.fori_loop(0, 2, far_a, 0)

    def attend_a(band, carry):
        rows, far = band_rows(band), band_rows(band + 2)
        bias_a[:, 0:BAND] = bias_s[rows, :]
        bias_a[:, BAND : 2 * BAND] = bias_of(xa[rows, 512:640], xa[far, 512:640], same[...])

        def pair_a(pair, inner):
            cut = lanes(pair)
            att[rows, cut] = attend_pair(
                qa[rows, cut],
                jnp.concatenate([ka[rows, cut], ka[far, cut]], axis=0),
                jnp.concatenate([va[rows, cut], va[far, cut]], axis=0),
                bias_a[...],
            )
            return inner

        lax.fori_loop(0, 4, pair_a, 0)
        o = dot(att[rows, :], tout[0])
        hidden = (xa[rows, 0:512].astype(F32) + o * normed(o)).astype(BF)
        hext[pl.ds(pl.multiple_of(band * BAND + HALF, 16), BAND), 0:512] = hidden
        return carry

    lax.fori_loop(0, 2, attend_a, 0)

    pack[...] = dot(gather[...], hext[HALF : HALF + TOK, :]).astype(BF)

    def section(sec, slot, device):
        piece = pl.ds(sec[0], sec[1])
        return copy_to(pack.at[piece], side_in.at[piece], slot, device)

    to_right = section(SEC_L, 1, (lat, right, grp))
    to_left = section(SEC_R, 2, (lat, left, grp))
    ups = (
        copy_to(
            hext.at[HALF : 2 * HALF],
            hext.at[HALF + TOK : 2 * HALF + TOK],
            3,
            (lat - 1, lon, grp),
        ),
        section(SEC_BL, 4, (lat - 1, right, grp)),
        section(SEC_BR, 5, (lat - 1, left, grp)),
    )
    downs = (
        copy_to(hext.at[TOK : TOK + HALF], hext.at[0:HALF], 6, (lat + 1, lon, grp)),
        section(SEC_TL, 7, (lat + 1, right, grp)),
        section(SEC_TR, 8, (lat + 1, left, grp)),
    )
    to_right.start()
    to_left.start()

    @pl.when(has_up)
    def _():
        for copy in ups:
            copy.start()

    @pl.when(has_down)
    def _():
        for copy in downs:
            copy.start()

    for layer in range(2):

        def forward(band, carry, layer=layer):
            rows = band_rows(band)
            source = hid[layer, rows, :]
            w = sqkv.at[layer]
            q = dot(source, w[:, 0:256]).astype(BF).astype(F32)
            rq = inverse_norm(q, heads[...])
            rq_s[layer, rows, :] = rq
            q_s[layer, rows, :] = (q * (rq * SCALE)).astype(BF)
            k = dot(source, w[:, 256:512]).astype(BF).astype(F32)
            rk = inverse_norm(k, heads[...])
            rk_s[layer, rows, :] = rk
            k_s[layer, rows, :] = (k * rk).astype(BF)
            v_s[layer, rows, :] = dot(source, w[:, 512:768]).astype(BF)
            bias = bias_s[rows, :]
            for pair in range(2):
                cut = slice(pair * 128, pair * 128 + 128)
                att_s[rows, cut] = attend_pair(
                    q_s[layer, rows, cut], k_s[layer, rows, cut], v_s[layer, rows, cut], bias
                )
            o = dot(att_s[rows, :], sout[layer])
            o_s[layer, rows, :] = o
            hidden = (source.astype(F32) + o * normed(o)).astype(BF)
            if layer == 0:
                hid[1, rows, :] = hidden
            else:
                pred[rows, :] = dot(hidden, sproj[...])
            return carry

        lax.fori_loop(0, 2, forward, 0)

    w_b = tqkv.at[1]

    def own_b(band, carry):
        rows = pl.ds(pl.multiple_of(band * BAND + HALF, 16), BAND)
        qa[band_rows(band), :] = project_queries(hext[rows, 0:512], w_b)
        project_keys(rows, hext, w_b, kb, vb, rows)
        return carry

    lax.fori_loop(0, 2, own_b, 0)
    to_right.wait()
    to_left.wait()

    @pl.when(has_up)
    def _():
        for copy in ups:
            copy.wait_send()
        for copy in downs:
            copy.wait_recv()

    @pl.when(has_down)
    def _():
        for copy in downs:
            copy.wait_send()
        for copy in ups:
            copy.wait_recv()

    side[...] = dot(spread[...], side_in[...]).astype(BF)
    for start in (0, HALF + TOK):
        rows = slice(start, start + HALF)
        project_keys(rows, hext, w_b, kb, vb, rows)

    def side_b(band, carry):
        rows = band_rows(band, SIDE)
        target = pl.ds(pl.multiple_of(band * SIDE + 3 * BAND, 16), SIDE)
        project_keys(rows, side, w_b, kb, vb, target)
        return carry

    lax.fori_loop(0, 3, side_b, 0)

    spans = ((HALF, HALF), (2 * HALF, BAND), (4 * HALF, HALF))
    at = 0
    for band, (start, size) in enumerate(spans):
        f_key = jnp.concatenate(
            [
                hext[band * BAND : (band + 1) * BAND, 512:640],
                side[band * SIDE : (band + 1) * SIDE, 512:640],
            ],
            axis=0,
        )
        bias_b[at : at + size, :] = bias_of(
            hext[start : start + size, 512:640], f_key, same_shifted[0:size, :]
        )
        at += size

    def pair_b(pair, carry):
        cut = lanes(pair)
        done = 0
        for band, (start, size) in enumerate(spans):
            mid = slice(band * BAND, (band + 1) * BAND)
            edge = slice(3 * BAND + band * SIDE, 3 * BAND + (band + 1) * SIDE)
            att[done : done + size, cut] = attend_pair(
                qa[done : done + size, cut],
                jnp.concatenate([kb[mid, cut], kb[edge, cut]], axis=0),
                jnp.concatenate([vb[mid, cut], vb[edge, cut]], axis=0),
                bias_b[done : done + size, :],
            )
            done += size
        return carry

    lax.fori_loop(0, 4, pair_b, 0)

    def finish_b(band, carry):
        rows = band_rows(band)
        o = dot(att[rows, :], tout[1])
        source = hext[pl.ds(pl.multiple_of(band * BAND + HALF, 16), BAND), 0:512]
        result = (source.astype(F32) + o * normed(o)).astype(BF)
        block = pl.ds(band * 12, 12)
        out_ref[block, :, :] = result.reshape(12, PADC, 512)[:, 0:COLS, :]
        residual = pred[rows, :] - result.astype(F32)
        g = dot_nt(residual.astype(BF), sproj[...]).astype(BF).astype(F32)
        bias = bias_s[rows, :]
        for layer in (1, 0):
            o = o_s[layer, rows, :]
            scale = normed(o)
            y = o * scale
            d_o = scale * (g - y * jnp.mean(g * y, axis=-1, keepdims=True))
            da_s[rows, :] = dot_nt(d_o.astype(BF), sout[layer]).astype(BF)
            for pair in range(2):
                cut = slice(pair * 128, pair * 128 + 128)
                dq, dk, dv = attend_pair_back(
                    q_s[layer, rows, cut],
                    k_s[layer, rows, cut],
                    v_s[layer, rows, cut],
                    da_s[rows, cut],
                    bias,
                )
                for piece, value in enumerate((dq, dk, dv)):
                    first = piece * 256 + pair * 128
                    dqkv[rows, first : first + 128] = value
            dq = dqkv[rows, 0:256] * SCALE
            q_hat = q_s[layer, rows, :].astype(F32) * (1.0 / SCALE)
            along = dot((q_hat * dq).astype(BF), heads[...])
            dq = (rq_s[layer, rows, :] * (dq - q_hat * along)).astype(BF)
            dk = dqkv[rows, 256:512]
            k_hat = k_s[layer, rows, :].astype(F32)
            along = dot((k_hat * dk).astype(BF), heads[...])
            dk = (rk_s[layer, rows, :] * (dk - k_hat * along)).astype(BF)
            dv = dqkv[rows, 512:768].astype(BF)
            w = sqkv.at[layer]
            back = (
                dot_nt(dq, w[:, 0:256]) + dot_nt(dk, w[:, 256:512]) + dot_nt(dv, w[:, 512:768])
            )
            g = g + back
            if layer == 1:
                g = g.astype(BF).astype(F32)
        grad_ref[block, :, :] = g.reshape(12, PADC, 256)[:, 0:COLS, :]
        return carry

    lax.fori_loop(0, 2, finish_b, 0)


def solution(mesh):
    n_lat, n_lon = mesh.shape["lat"], mesh.shape["lon"]

    def shards(teacher_in, student_in, regions, t_qkv, t_out, s_qkv, s_out, s_proj):
        assert teacher_in.shape == (1, ROWS, COLS, 512)
        vm = pl.BlockSpec(memory_space=pltpu.VMEM)
        scratch = [
            ((ROWS, PADC, 512), BF),
            ((ROWS, PADC, 256), BF),
            ((128, 128), F32),
            ((2 * TOK, 640), BF),
            ((TOK, 512), BF),
            ((2 * TOK, 512), BF),
            ((2 * TOK, 512), BF),
            ((BAND, 2 * BAND), F32),
            ((TOK, BAND), F32),
            ((TOK, BAND + SIDE), F32),
            ((TOK, 512), BF),
            ((TOK + 2 * HALF, 640), BF),
            ((PACK, 640), BF),
            ((PACK, 640), BF),
            ((PACK, 640), BF),
            ((3 * BAND + 3 * SIDE, 512), BF),
            ((3 * BAND + 3 * SIDE, 512), BF),
            ((2, TOK, 256), BF),
            ((2, TOK, 256), BF),
            ((2, TOK, 256), BF),
            ((2, TOK, 256), BF),
            ((2, TOK, 256), F32),
            ((2, TOK, 256), F32),
            ((2, TOK, 256), F32),
            ((TOK, 256), BF),
            ((TOK, 512), F32),
            ((TOK, 256), BF),
            ((TOK, 768), F32),
        ]
        operands = (
            teacher_in[0],
            student_in[0],
            regions,
            t_qkv,
            t_out,
            s_qkv,
            s_out,
            s_proj,
        ) + constants()
        teacher_out, grad = pl.pallas_call(
            functools.partial(kernel, n_lat, n_lon),
            out_shape=(
                jax.ShapeDtypeStruct((ROWS, COLS, 512), BF),
                jax.ShapeDtypeStruct((ROWS, COLS, 256), F32),
            ),
            in_specs=[vm] * len(operands),
            out_specs=(vm, vm),
            scratch_shapes=[pltpu.VMEM(shape, kind) for shape, kind in scratch]
            + [pltpu.SemaphoreType.DMA((9,)), pltpu.SemaphoreType.DMA((9,))],
            compiler_params=pltpu.CompilerParams(
                collective_id=0, has_side_effects=True, vmem_limit_bytes=60 * 1024 * 1024
            ),
        )(*operands)
        return teacher_out[None], grad[None]

    return jax.shard_map(
        shards,
        mesh=mesh,
        in_specs=(
            P("grp", "lat", "lon", None),
            P("grp", "lat", "lon", None),
            P(None, "lat", "lon"),
            P(),
            P(),
            P(),
            P(),
            P(),
        ),
        out_specs=(P("grp", "lat", "lon", None), P("grp", "lat", "lon", None)),
        check_vma=False,
    )
```

time: 147 us -> 49.1 us (0.33)
  matrix products: 45.5 us -> 0 us
  local copies, waits for them, and re-layouts: 51.9 us -> 8.57 us
  Pallas kernels: 0 us -> 39.6 us
  waiting for transfers between devices: 16.8 us -> 0 us
  other arithmetic: 16.5 us -> 0 us
  starting transfers between devices: 12.2 us -> 0 us
  between operations: 2.64 us -> 0.64 us
    dot_general x41 -> x0, matrix products: 45.5 us -> none  [the longest x9 19.3 us: band_attend(): jnp.einsum('bqhd,bkhd->bhqk', q_heads, k_heads, preferred_element_type=jn...]
    pallas_call x0 -> x1, Pallas kernels: none -> 39.6 us  [shards(): pl.pallas_call(functools.partial(kernel, n_lat, n_lon), out_shape=(jax.Sh...]
    ppermute x9 -> x0, waiting for transfers between devices: 16.8 us -> none  [the longest x4 11.5 us: padded(): after = lax.ppermute(first, axis, down)]
    ppermute x9 -> x0, starting transfers between devices: 12.2 us -> none  [the longest x4 8.16 us: padded(): after = lax.ppermute(first, axis, down)]
    another operation x14 -> x0, local copies, waits for them, and re-layouts: 10.1 us -> none  [the longest x6 3.93 us: head_split(): heads = source.reshape(bands, count, head_count, channels // head_count)]
    slice x16 -> x0, local copies, waits for them, and re-layouts: 8.41 us -> none  [the longest x4 2.41 us: padded(): first = lax.slice_in_dim(shard, 0, width, axis=dim)]
    reduce_sum x11 -> x0, other arithmetic: 7.22 us -> none  [the longest x9 5.11 us: head_split(): jnp.sum(jnp.square(heads.astype(jnp.float32)), axis=3) + eps]
    reshape x30 -> x0, local copies, waits for them, and re-layouts: 6.78 us -> none  [the longest x9 3.36 us: project(): return result.reshape(source.shape[:-1] + (matrix.shape[1],))]
  transfers between devices with their start and end apart: 9 -> 0, of which waited for: 5 -> 0; matrix products, arithmetic and copies ran while one was open for 26% -> 0% of each run, Pallas kernels for 0% -> 0%
where the time goes in v1:
time: 49.1 us; the launch traced here: 48.8 us
  Pallas kernels  39.6 us (81%)
  local copies, waits for them, and re-layouts  8.57 us (17%)
  between operations  0.64 us (1%)
    pallas_call x1, Pallas kernels, shards(): pl.pallas_call(functools.partial(kernel, n_lat, n_lon), out_shape=(jax.Sh...  39.6 us
    unnamed x5, local copies, waits for them, and re-layouts  8.57 us

profile of v1, /device:TPU:0, one launch (start us, length us, event | category | flops | bytes accessed | tf_op | source)
XLA Modules:
  0.0 48.8 jit_solution(14074188491399447111)
XLA Ops:
  0.6 1.4 %copy.19.reg_ref = s32[2,24,12]{2,1,0:T(8,128)} copy(s32[2,24,12]{1,0,2:T(2,128)} %param.17) | data formatting | bytes 4608 | tf_op args[2]
  2.0 1.6 %copy.25 = bf16[1,24,12,256]{3,2,1,0:T(8,128)(2,1)} copy(bf16[1,24,12,256]{3,1,2,0:T(8,128)(2,1)} %param.16) | data formatting | bytes 294912 | tf_op args[1]
  3.6 1.8 %copy.24 = bf16[1,24,12,512]{3,2,1,0:T(8,128)(2,1)} copy(bf16[1,24,12,512]{3,1,2,0:T(8,128)(2,1)} %param.15) | data formatting | bytes 589824 | tf_op args[0]
  5.4 39.6 %shard_map.158 = (bf16[24,12,512]{2,1,0:T(8,128)(2,1)}, f32[24,12,256]{2,1,0:T(8,128)}) custom-call(bf16[24,12,512]{2,1,0:T(8,128)(2,1)} %bitcast.8, bf16[24,12,256]{2,1,0:T(8,128)(2,1)} %bitcast.9, s32[2,24,12]{2,1,0:T(8,128)} %copy.19.reg_ref, bf16[2,512,1536]{2,1,0:T(8,128)(2,1)} %tqkv.1, bf16[2,512,512]{2,1,0:T(8,128)(2,1)} %tout.1, ...), custom_call_target="tpu_custom_call" | custom-call | tf_op jit(solution)/shard_map/pallas_call | solution.py:573
  45.0 1.9 %copy.20 = bf16[1,24,12,512]{3,1,2,0:T(8,128)(2,1)} copy(bf16[1,24,12,512]{3,2,1,0:T(8,128)(2,1)} %bitcast.11) | data formatting | bytes 589824
  46.9 1.9 %copy.21 = f32[1,24,12,256]{3,1,2,0:T(8,128)} copy(f32[1,24,12,256]{3,2,1,0:T(8,128)} %bitcast.10) | data formatting | bytes 589824
